TPU v7x, 128 devices: a whole 4x4x4 slice. The times are simulated.
128 devices in a mesh: seq: 64 (over z, x, y_hi, core), ch: 2 (over y_lo).
Axes of the slice: x: 4, y: 4 (y_hi: 2, y_lo: 2; y = y_hi * 2 + y_lo), z: 4, core: 2. Of those that a mesh axis runs over, the one named last changes fastest.
Arguments:
- inputs: bfloat16 [2, 65536, 1536], P(None, 'seq', 'ch'), may hold values from -6 to 6
- cotangent: bfloat16 [2, 65536, 1536], P(None, 'seq', 'ch'), may hold values from -6 to 6
- conv_out: bfloat16 [2, 65536, 768], P(None, 'seq'), may hold values from -6 to 6
- conv_weight: bfloat16 [3, 1536, 768], P(None, 'ch'), may hold values from -0.09375 to 0.09375
- proj_weight: bfloat16 [768, 1536], P(None, 'ch'), may hold values from -0.21875 to 0.21875
Outputs:
- grad_inputs: bfloat16 [2, 65536, 1536], P(None, 'seq', 'ch')
- grad_conv: bfloat16 [3, 1536, 768], P(None, 'ch')
- grad_proj: bfloat16 [768, 1536], P(None, 'ch')
All inputs are finite; a program needn't handle non-finite values.
Results may differ from a plain program's by a relative error of at most 0.0061.
Values may be sent and summed in bfloat16 or wider, within the bound.
A program may use at most 128 MiB of HBM per device.

v0:
```python
import math

import jax
import jax.numpy as jnp
from jax import lax
from jax.sharding import PartitionSpec as P

DILATION_STEP = 2048


def shifted(value, axis, steps):
    count = lax.axis_size(axis)
    leading, last = (max(0, -steps), min(count, count - steps))
    return lax.ppermute(value, axis, [(source, source + steps) for source in range(leading, last)])


def contract_rows(left, right):
    return lax.dot_general(
        left, right, (((0,), (0,)), ((), ())), preferred_element_type=jnp.float32
    )


def gelu_parts(values):
    wide = values.astype(jnp.float32)
    cumul = 0.5 * (1.0 + jax.scipy.special.erf(wide / math.sqrt(2.0)))
    dense = jnp.exp(-0.5 * wide * wide) / math.sqrt(2.0 * math.pi)
    return (wide * cumul, cumul + wide * dense)


def shards(inputs, cotangent, conv_out, conv_weight, proj_weight):
    batches, sequence_length, chan_part = inputs.shape
    inner_width = conv_out.shape[2]
    row_count = batches * sequence_length
    flat_g = cotangent.reshape(row_count, chan_part)
    partial_mid = jnp.dot(flat_g, proj_weight.T, preferred_element_type=jnp.float32)
    summed_mid = lax.psum(partial_mid, "ch")
    middle_gradient = summed_mid.astype(jnp.bfloat16).reshape(batches, sequence_length, inner_width)
    neighbor_hops = DILATION_STEP // sequence_length
    following = shifted(middle_gradient, "seq", -neighbor_hops)
    preceding = shifted(middle_gradient, "seq", neighbor_hops)
    tap_list = (
        following.reshape(row_count, inner_width),
        middle_gradient.reshape(row_count, inner_width),
        preceding.reshape(row_count, inner_width),
    )
    grad_hidden = jnp.zeros((row_count, chan_part), jnp.float32)
    for tap_index in range(3):
        grad_hidden = grad_hidden + jnp.dot(
            tap_list[tap_index], conv_weight[tap_index].T, preferred_element_type=jnp.float32
        )
    hidden_full, deriv = gelu_parts(inputs.reshape(row_count, chan_part))
    hidden = hidden_full.astype(jnp.bfloat16)
    grad_inputs = (flat_g.astype(jnp.float32) + grad_hidden * deriv).astype(jnp.bfloat16)
    grad_inputs = grad_inputs.reshape(batches, sequence_length, chan_part)
    grad_scale = 1.0 / math.sqrt(float(row_count * lax.axis_size("seq")))
    conv_terms = jnp.stack(
        [contract_rows(hidden, tap_list[tap_index]) * grad_scale for tap_index in range(3)]
    )
    proj_terms = contract_rows(conv_out.reshape(row_count, inner_width), flat_g) * grad_scale
    conv_total, proj_total = lax.psum((conv_terms, proj_terms), "seq")
    return (grad_inputs, conv_total.astype(jnp.bfloat16), proj_total.astype(jnp.bfloat16))


def solution(mesh):
    in_specs = (
        P(None, "seq", "ch"),
        P(None, "seq", "ch"),
        P(None, "seq", None),
        P(None, "ch", None),
        P(None, "ch"),
    )
    out_specs = (P(None, "seq", "ch"), P(None, "ch", None), P(None, "ch"))
    return jax.shard_map(shards, mesh=mesh, in_specs=in_specs, out_specs=out_specs, check_vma=False)
```

profile of v0, /device:TPU:1, one launch (start us, length us, event | category | flops | bytes accessed | tf_op | source)
XLA Modules:
  0.0 696.0 jit_solution(10845579516698475319)
XLA Ops:
  0.6 0.0 copy-start
  0.6 7.7 %fusion.29 = f32[2048,768]{1,0:T(8,128)} fusion(bf16[2048,768]{1,0:T(8,128)(2,1)} %bitcast.60, bf16[768,768]{1,0:T(8,128)(2,1)} %param.9), kind=kOutput, calls=%fused_computation.36 | convolution fusion | flops 2415919104 | bytes 10616832 | tf_op jit(solution)/shard_map/dot_general | solution.py:35
  8.3 147.3 %all-reduce.3 = bf16[2048,768]{1,0:T(8,128)(2,1)} all-reduce(f32[2048,768]{1,0:T(8,128)} %fusion.29), channel_id=1, replica_groups=mesh['seq'=64,'ch'=2] {'ch'}, use_global_device_ids=true, to_apply=%region_0.0 | all-reduce | flops 1572864 | bytes 9437184 | tf_op jit(solution)/shard_map/psum | solution.py:36
  155.6 0.0 copy-start.3
  155.6 0.0 copy-start.5
  155.6 1.5 collective-permute-start
  157.2 5.8 collective-permute-start.1
  163.0 0.0 copy-done
  163.0 6.0 bitcast_multiply_fusion.2
  169.0 0.0 copy-done.3
  169.0 0.0 copy-done.5
  169.0 0.0 copy-start.2
  169.0 4.8 fusion.21
  173.8 0.0 copy-done.2
  173.8 1.6 fusion.10
  175.4 4.0 fusion.14
  179.4 2.7 multiply_bitcast_fusion
  182.1 112.4 %collective-permute-done = bf16[2,1024,768]{2,1,0:T(8,128)(2,1)S(1)} collective-permute-done((bf16[2,1024,768]{2,1,0:T(8,128)(2,1)}, bf16[2,1024,768]{2,1,0:T(8,128)(2,1)S(1)}, u32[]{:S(2)}, u32[]{:S(2)}) %collective-permute-start) | collective-permute-done | bytes 3145760 | tf_op jit(solution)/shard_map/ppermute | solution.py:14
  294.5 4.5 fusion.23
  299.1 2.7 fusion.16
  301.8 0.0 collective-permute-done.1
  301.8 0.0 copy-start.4
  301.8 1.6 copy-done.4
  303.4 2.7 fusion.15
  306.1 3.4 pad_maximum_fusion
  309.5 370.9 %all-reduce.4 = (bf16[3,768,768]{2,1,0:T(8,128)(2,1)}, bf16[768,768]{1,0:T(8,128)(2,1)}) all-reduce(f32[3,768,768]{2,1,0:T(8,128)} %pad_maximum_fusion, f32[768,768]{1,0:T(8,128)} %bitcast_multiply_fusion.2), channel_id=1, replica_groups=mesh['seq'=64,'ch'=2] {'seq'}, use_global_device_ids=true, to_apply=%region_1.0 | all-reduce | flops 2359296 | bytes 14155776 | tf_op jit(solution)/shard_map/psum | solution.py:60
  680.4 0.0 copy-start.1
  680.4 15.6 %fusion.6 = bf16[2048,768]{1,0:T(8,128)(2,1)} fusion(f32[2048,768]{1,0:T(8,128)} %get-tuple-element.6, bf16[2,1024,768]{2,1,0:T(8,128)(2,1)} %param.5, f32[2048,768]{1,0:T(8,128)} %fusion.23, f32[2048,768]{1,0:T(8,128)} %fusion.21, bf16[2048,768]{1,0:T(8,128)(2,1)} %bitcast.61, bf16[2048,768]{1,0:T(8,128)(2,1)} %bitcast.62, bf16[3,768,768]{2,1,0:T(8,128)(2,1)} %param.8), kind=kOutput, calls=%fused_computation.8 | convolution fusion | flops 2434793472 | bytes 32636928 | tf_op jit(solution)/shard_map/dot_general | solution.py:48
  696.0 0.0 copy-done.1
Async XLA Ops:
  0.6 162.4 %copy-start = (bf16[2,1024,768]{2,1,0:T(8,128)(2,1)S(1)}, bf16[2,1024,768]{2,1,0:T(8,128)(2,1)}, u32[]{:S(2)}) copy-start(bf16[2,1024,768]{2,1,0:T(8,128)(2,1)} %param.7) | copy-start | bytes 9437188
  155.6 13.4 %copy-start.3 = (bf16[2048,768]{1,0:T(8,128)(2,1)S(1)}, bf16[2048,768]{1,0:T(8,128)(2,1)}, u32[]{:S(2)}) copy-start(bf16[2048,768]{1,0:T(8,128)(2,1)} %all-reduce.3) | copy-start | bytes 9437188
  155.6 13.4 %copy-start.5 = (bf16[3,768,768]{2,1,0:T(8,128)(2,1)S(1)}, bf16[3,768,768]{2,1,0:T(8,128)(2,1)}, u32[]{:S(2)}) copy-start(bf16[3,768,768]{2,1,0:T(8,128)(2,1)} %param.8) | copy-start | bytes 10616836
  155.6 138.9 %collective-permute-start = (bf16[2,1024,768]{2,1,0:T(8,128)(2,1)}, bf16[2,1024,768]{2,1,0:T(8,128)(2,1)S(1)}, u32[]{:S(2)}, u32[]{:S(2)}) collective-permute-start(bf16[2,1024,768]{2,1,0:T(8,128)(2,1)} %bitcast.58), channel_id=1, source_target_pairs={{4,0},{6,2},{8,4},{10,6},{12,8},{14,10},{16,12},{18,14},{20,16},{2... | collective-permute-start | bytes 9437192 | tf_op jit(solution)/shard_map/ppermute | solution.py:14
  157.2 144.6 %collective-permute-start.1 = (bf16[2,1024,768]{2,1,0:T(8,128)(2,1)}, bf16[2,1024,768]{2,1,0:T(8,128)(2,1)S(1)}, u32[]{:S(2)}, u32[]{:S(2)}) collective-permute-start(bf16[2,1024,768]{2,1,0:T(8,128)(2,1)} %bitcast.59), channel_id=1, source_target_pairs={{0,4},{2,6},{4,8},{6,10},{8,12},{10,14},{12,16},{14,18},{16,20},{1... | collective-permute-start | bytes 9437192 | tf_op jit(solution)/shard_map/ppermute | solution.py:14
  169.0 4.8 copy-start.2
  301.8 1.6 copy-start.4
  680.4 15.6 %copy-start.1 = (bf16[2,1024,768]{2,1,0:T(8,128)(2,1)S(1)}, bf16[2,1024,768]{2,1,0:T(8,128)(2,1)}, u32[]{:S(2)}) copy-start(bf16[2,1024,768]{2,1,0:T(8,128)(2,1)} %param.7) | copy-start | bytes 9437188
where the time goes:
time: 703 us; the launch traced here: 696 us
  blocking collectives  518 us (74%)
  waiting for transfers between devices  112 us (16%)
  matrix products  46.7 us (7%)
  other arithmetic  8.96 us (1%)
  starting transfers between devices  7.37 us (1%)
    psum x1, blocking collectives, shards(): conv_total, proj_total = lax.psum((conv_terms, proj_terms), 'seq')  371 us
    psum x1, blocking collectives, shards(): summed_mid = lax.psum(partial_mid, 'ch')  147 us
    ppermute x2, waiting for transfers between devices, shifted(): lax.ppermute(value, axis, [(source, source + steps) for source in range(l...  112 us
    dot_general x3, matrix products, shards(): jnp.dot(tap_list[tap_index], conv_weight[tap_index].T, preferred_element_...  24.8 us
    dot_general x4, matrix products, contract_rows(): lax.dot_general(left, right, (((0,), (0,)), ((), ())), preferred_element_...  14.2 us
  transfers between devices with their start and end apart: 2, of which 1 were waited for; matrix products, arithmetic and copies ran while one was open for 4% of the time, Pallas kernels for 0%

commit v1 on v0

v1 whole, which is shorter than its diff:
```python
import functools
import math

import jax
import jax.numpy as jnp
from jax import lax
from jax.experimental import pallas as pl
from jax.experimental.pallas import tpu as pltpu
from jax.sharding import PartitionSpec as P

MESH = pl.DeviceIdType.MESH
ROWS = 2048
CH = 768
FULL = 768
FW = 256
NF = FULL // FW
RB = 256
NB = ROWS // RB
NT = NF * NB
WINDOW = 6
LAG = 2
SLAB = 3 * CH
ZP = SLAB // 4
XP = ZP // 8
SCALE = 1.0 / math.sqrt(131072.0)
BF = jnp.bfloat16
F32 = jnp.float32


def dot(a, b):
    return lax.dot_general(a, b, (((1,), (0,)), ((), ())), preferred_element_type=F32)


def dot_t(a, b):
    return lax.dot_general(a, b, (((1,), (1,)), ((), ())), preferred_element_type=F32)


def wait_for(ref, sem):
    pltpu.make_async_copy(ref, ref, sem).wait()


def kernel(
    inp_h, cot_h, cout_h, cw_h, pw_h, gi_h, wg_h,
    cot, io, h_t, der, pw, cw, part, mid, mid_q, mid_x, gh,
    slab, own32, z32, cs, cr, zs, zr, xs, xr, fin,
    ld_sem, out_sem, wout_sem,
    e_send, e_recv, q_send, q_recv, x_send, x_recv,
    c_send, c_recv, zz_send, zz_recv, xy_send, xy_recv,
    axy_send, axy_recv, az_send, az_recv, ac_send, ac_recv,
):
    s = lax.axis_index("seq")
    c = lax.axis_index("ch")
    core = s % 2
    yh = (s // 2) % 2
    p = (s // 2) % 8
    z = s // 16

    def dev(seq, ch):
        return {"seq": seq, "ch": ch}

    partner = dev(s, 1 - c)
    across = dev(s + 2 - 4 * yh, 1 - c)
    ahead = s + 4 - 8 * yh
    behind = s - 4 + 8 * yh
    has_dst = jnp.logical_and(ahead >= 0, ahead < 64)
    has_src = jnp.logical_and(behind >= 0, behind < 64)
    twin = dev(s + 1 - 2 * core, c)

    def z_peer(d):
        return (z + d) % 4

    def z_dev(d):
        return dev(z_peer(d) * 16 + s % 16, c)

    def p_peer(d):
        return (p + d) % 8

    def p_dev(d):
        return dev(z * 16 + p_peer(d) * 2 + core, c)

    ld_cot = pltpu.make_async_copy(cot_h, cot, ld_sem.at[0])
    ld_pw = pltpu.make_async_copy(pw_h, pw, ld_sem.at[1])
    ld_cout = pltpu.make_async_copy(cout_h, io, ld_sem.at[2])
    ld_inp = pltpu.make_async_copy(inp_h, io, ld_sem.at[3])
    ld_cw = [
        pltpu.make_async_copy(cw_h.at[:, :, pl.ds(f * FW, FW)], cw.at[f], ld_sem.at[4 + f])
        for f in range(NF)
    ]
    ld_cot.start()
    ld_pw.start()
    ld_cout.start()
    for cp in ld_cw:
        cp.start()

    barrier = pltpu.get_barrier_semaphore()

    def greet(device):
        pl.semaphore_signal(barrier, inc=1, device_id=device, device_id_type=MESH)

    greet(partner)
    greet(across)
    greet(twin)
    for d in range(1, 4):
        greet(z_dev(d))
    for d in range(1, 8):
        greet(p_dev(d))

    far_dst = jnp.logical_and(has_dst, ahead // 16 != z)
    far_src = jnp.logical_and(has_src, behind // 16 != z)

    @pl.when(far_dst)
    def _():
        greet(dev(ahead, c))

    @pl.when(far_src)
    def _():
        greet(dev(behind, c))

    pl.semaphore_wait(barrier, 13 + far_dst.astype(jnp.int32) + far_src.astype(jnp.int32))

    def block(ref, t):
        return ref.at[t // NB, pl.ds(pl.multiple_of((t % NB) * RB, RB), RB)]

    def start_e(t):
        pltpu.make_async_remote_copy(
            src_ref=block(part, t), dst_ref=block(mid, t), send_sem=e_send, recv_sem=e_recv.at[t],
            device_id=partner, device_id_type=MESH,
        ).start()

    def start_q(t):
        pltpu.make_async_remote_copy(
            src_ref=block(mid, t), dst_ref=block(mid_q, t), send_sem=q_send, recv_sem=q_recv.at[t],
            device_id=across, device_id_type=MESH,
        ).start()

    def forward_x(t):
        wait_for(block(mid_q, t), q_recv.at[t])

        @pl.when(has_dst)
        def _():
            pltpu.make_async_remote_copy(
                src_ref=block(mid_q, t), dst_ref=block(mid_x, t), send_sem=x_send, recv_sem=x_recv.at[t // NB],
                device_id=dev(ahead, c), device_id_type=MESH,
            ).start()

    ld_cot.wait()
    ld_pw.wait()

    def part_chunk(f, _):
        weights = pw[pl.ds(pl.multiple_of(f * FW, FW), FW), :]

        def part_block(r, _):
            rows = pl.ds(pl.multiple_of(r * RB, RB), RB)
            part[f, rows, :] = dot_t(cot[rows, :], weights).astype(BF)
            t = f * NB + r

            @pl.when(t < WINDOW)
            def _():
                start_e(t)

            return 0

        return lax.fori_loop(0, NB, part_block, 0)

    lax.fori_loop(0, NF, part_chunk, 0)

    @pl.when(jnp.logical_not(has_src))
    def _():
        def clear(i, _):
            mid_x[i // 32, pl.ds(pl.multiple_of((i % 32) * 64, 64), 64), :] = jnp.zeros((64, FW), BF)
            return 0

        lax.fori_loop(0, 32 * NF, clear, 0)

    def service(t):
        wait_for(block(mid, t), e_recv.at[t])
        nxt = t + WINDOW

        @pl.when(nxt < NT)
        def _():
            start_e(nxt)

        f, r0 = t // NB, (t % NB) * RB

        def add(i, _):
            rows = pl.ds(pl.multiple_of(r0 + i * 64, 64), 64)
            mid[f, rows, :] = (part[f, rows, :].astype(F32) + mid[f, rows, :].astype(F32)).astype(BF)
            return 0

        lax.fori_loop(0, RB // 64, add, 0)
        start_q(t)

    def store_slab(row, value):
        rows = pl.ds(pl.multiple_of(row, 256), 256)
        slab[0, rows, :] = value[:, :128]
        slab[1, rows, :] = value[:, 128:]

    ld_cout.wait()

    def turn(i, _):
        span = pl.ds(pl.multiple_of(i * 128, 128), 128)
        h_t[:, span] = io[span, :].T
        return 0

    lax.fori_loop(0, ROWS // 128, turn, 0)
    ld_inp.start()
    for k in range(3):
        def proj_tile(i, _, k=k):
            rows = pl.ds(pl.multiple_of(i * 256, 256), 256)
            store_slab(k * CH + i * 256, dot(h_t[rows, :], cot[:, k * 256:(k + 1) * 256]))
            return 0

        lax.fori_loop(0, 3, proj_tile, 0)

    def core_send(g):
        def cast(i, _):
            rows = pl.ds(pl.multiple_of(i * 64, 64), 64)
            cs[g, rows, :] = slab[1 - core, rows, :].astype(BF)
            return 0

        lax.fori_loop(0, SLAB // 64, cast, 0)
        pltpu.make_async_remote_copy(
            src_ref=cs.at[g], dst_ref=cr.at[g], send_sem=c_send, recv_sem=c_recv.at[g],
            device_id=twin, device_id_type=MESH,
        ).start()

    def z_send(g):
        wait_for(cr.at[g], c_recv.at[g])

        def add(i, _):
            rows = pl.ds(pl.multiple_of(i * 64, 64), 64)
            total = slab[core, rows, :] + cr[g, rows, :].astype(F32)
            slab[core, rows, :] = total
            zs[g, i // (ZP // 64), pl.ds(pl.multiple_of((i % (ZP // 64)) * 64, 64), 64), :] = total.astype(BF)
            return 0

        lax.fori_loop(0, SLAB // 64, add, 0)
        own32[...] = slab[core, pl.ds(pl.multiple_of(z * ZP, 64), ZP), :]
        for d in range(1, 4):
            pltpu.make_async_remote_copy(
                src_ref=zs.at[g, z_peer(d)], dst_ref=zr.at[g, d - 1], send_sem=zz_send, recv_sem=zz_recv.at[g],
                device_id=z_dev(d), device_id_type=MESH,
            ).start()

    def x_send_sum(g):
        wait_for(zr.at[g], zz_recv.at[g])

        def add(i, _):
            rows = pl.ds(pl.multiple_of(i * 64, 64), 64)
            z32[rows, :] = (own32[rows, :] + zr[g, 0, rows, :].astype(F32)) + (
                zr[g, 1, rows, :].astype(F32) + zr[g, 2, rows, :].astype(F32)
            )
            return 0

        lax.fori_loop(0, ZP // 64, add, 0)
        for i in range(8):
            xs[g, i] = z32[i * XP:(i + 1) * XP, :].astype(BF)
        for d in range(1, 8):
            pltpu.make_async_remote_copy(
                src_ref=xs.at[g, p_peer(d)], dst_ref=xr.at[g, d - 1], send_sem=xy_send, recv_sem=xy_recv.at[g],
                device_id=p_dev(d), device_id_type=MESH,
            ).start()

    def finish(g):
        wait_for(xr.at[g], xy_recv.at[g])
        total = z32[pl.ds(pl.multiple_of(p * XP, 8), XP), :]
        for d in range(7):
            total = total + xr[g, d].astype(F32)
        fin[g, core, z, p] = (total * SCALE).astype(BF)
        for d in range(1, 8):
            piece = fin.at[g, core, z, p]
            pltpu.make_async_remote_copy(
                src_ref=piece, dst_ref=piece, send_sem=axy_send, recv_sem=axy_recv.at[g],
                device_id=p_dev(d), device_id_type=MESH,
            ).start()

    def gather_z(g):
        wait_for(xr.at[g], axy_recv.at[g])
        for d in range(1, 4):
            piece = fin.at[g, core, z]
            pltpu.make_async_remote_copy(
                src_ref=piece, dst_ref=piece, send_sem=az_send, recv_sem=az_recv.at[g],
                device_id=z_dev(d), device_id_type=MESH,
            ).start()

    def gather_core(g):
        wait_for(fin.at[g, core, pl.ds(0, 3)], az_recv.at[g])
        piece = fin.at[g, core]
        pltpu.make_async_remote_copy(
            src_ref=piece, dst_ref=piece, send_sem=ac_send, recv_sem=ac_recv.at[g],
            device_id=twin, device_id_type=MESH,
        ).start()

    def write_out(g):
        wait_for(fin.at[g, 1 - core], ac_recv.at[g])
        pltpu.make_async_copy(fin.at[g], wg_h.at[g], wout_sem).start()

    core_send(0)

    def gelu(i):
        def tile(j, _):
            rows = pl.ds(pl.multiple_of(i * RB + j * 128, 128), 128)

            def strip(m, _):
                sub = pl.ds(pl.multiple_of(i * RB + j * 128 + m * 16, 16), 16)
                wide = io[sub, :].astype(F32)
                cumul = 0.5 * (1.0 + lax.erf(wide * (1.0 / math.sqrt(2.0))))
                dense = jnp.exp(-0.5 * wide * wide) * (1.0 / math.sqrt(2.0 * math.pi))
                der[sub, :] = cumul + wide * dense
                io[sub, :] = (wide * cumul).astype(BF)
                return 0

            lax.fori_loop(0, 8, strip, 0)
            h_t[:, rows] = io[rows, :].T
            return 0

        lax.fori_loop(0, RB // 128, tile, 0)

    ld_inp.wait()
    for i in range(NB):
        service(i)
        if i >= LAG:
            forward_x(i - LAG)
        if i == 2:
            z_send(0)
        if i == 4:
            x_send_sum(0)
        if i == 6:
            finish(0)
        gelu(i)

    for cp in ld_cw:
        cp.wait()

    tap_q = 2 * yh
    tap_x = 2 - 2 * yh

    def weight_tap(f, tap, taps):
        def tile(i, _):
            rows = pl.ds(pl.multiple_of(i * 256, 256), 256)
            store_slab(tap * CH + i * 256, dot(h_t[rows, :], taps[f]))
            return 0

        lax.fori_loop(0, CH // 256, tile, 0)

    def data_rows(g, first, count):
        f = g - 1

        def tile(i, _):
            rows = pl.ds(pl.multiple_of(i * RB, RB), RB)
            total = dot_t(mid[f, rows, :], cw[f, 1])
            total = total + dot_t(mid_q[f, rows, :], cw[f, tap_q])
            total = total + dot_t(mid_x[f, rows, :], cw[f, tap_x])

            @pl.when(g == 1)
            def _():
                gh[rows, :] = total

            @pl.when(g > 1)
            def _():
                gh[rows, :] = gh[rows, :] + total

            @pl.when(g == NF)
            def _():
                def strip(m, _):
                    sub = pl.ds(pl.multiple_of(i * RB + m * 16, 16), 16)
                    io[sub, :] = (cot[sub, :].astype(F32) + gh[sub, :] * der[sub, :]).astype(BF)
                    return 0

                lax.fori_loop(0, RB // 16, strip, 0)
                pltpu.make_async_copy(io.at[rows], gi_h.at[rows], out_sem).start()

            return 0

        lax.fori_loop(first, first + count, tile, 0)

    def phase(g, _):
        f = g - 1

        def serve(i):
            t = g * NB + i

            @pl.when(g < NF)
            def _():
                service(t)

            if i < LAG:
                forward_x(t - LAG)
            else:
                @pl.when(g < NF)
                def _():
                    forward_x(t - LAG)

        serve(0)
        gather_z(g - 1)
        weight_tap(f, 1, mid)
        serve(1)
        weight_tap(f, tap_q, mid_q)
        serve(2)
        gather_core(g - 1)
        serve(3)

        @pl.when(has_src)
        def _():
            wait_for(mid_x.at[f], x_recv.at[f])

        weight_tap(f, tap_x, mid_x)
        core_send(g)
        serve(4)
        data_rows(g, 0, NB // 2)
        serve(5)
        z_send(g)
        write_out(g - 1)
        data_rows(g, NB // 2, NB // 4)
        serve(6)
        x_send_sum(g)
        data_rows(g, NB // 2 + NB // 4, NB // 4)
        serve(7)
        finish(g)
        return 0

    lax.fori_loop(1, NF + 1, phase, 0)
    gather_z(NF)
    gather_core(NF)
    write_out(NF)

    wait_for(part, e_send)
    wait_for(mid, q_send)

    @pl.when(has_dst)
    def _():
        wait_for(mid_q, x_send)

    wait_for(cs, c_send)
    wait_for(zr, zz_send)
    wait_for(xr, xy_send)
    wait_for(xr, axy_send)
    for g in range(NF + 1):
        wait_for(fin.at[g, 0, pl.ds(0, 3)], az_send)
        wait_for(fin.at[g, 0], ac_send)
    wait_for(io, out_sem)
    wait_for(fin, wout_sem)


def shards(inputs, cotangent, conv_out, conv_weight, proj_weight):
    any_spec = pl.BlockSpec(memory_space=pl.ANY)
    dma = pltpu.SemaphoreType.DMA
    slabs = NF + 1
    rows_bf = pltpu.VMEM((ROWS, CH), BF)
    chunks = pltpu.VMEM((NF, ROWS, FW), BF)
    flat = [a.reshape(ROWS, CH) for a in (inputs, cotangent, conv_out)]
    grad_inputs, raw = pl.pallas_call(
        kernel,
        out_shape=(
            jax.ShapeDtypeStruct((ROWS, CH), BF),
            jax.ShapeDtypeStruct((slabs, 2, 4, 8, XP, 128), BF),
        ),
        in_specs=[any_spec] * 5,
        out_specs=(any_spec, any_spec),
        scratch_shapes=[
            rows_bf, rows_bf, pltpu.VMEM((CH, ROWS), BF), pltpu.VMEM((ROWS, CH), F32),
            pltpu.VMEM((FULL, CH), BF), pltpu.VMEM((NF, 3, CH, FW), BF),
            chunks, chunks, chunks, chunks, pltpu.VMEM((ROWS, CH), F32),
            pltpu.VMEM((2, SLAB, 128), F32), pltpu.VMEM((ZP, 128), F32), pltpu.VMEM((ZP, 128), F32),
            pltpu.VMEM((slabs, SLAB, 128), BF), pltpu.VMEM((slabs, SLAB, 128), BF),
            pltpu.VMEM((slabs, 4, ZP, 128), BF), pltpu.VMEM((slabs, 3, ZP, 128), BF),
            pltpu.VMEM((slabs, 8, XP, 128), BF), pltpu.VMEM((slabs, 7, XP, 128), BF),
            pltpu.VMEM((slabs, 2, 4, 8, XP, 128), BF),
            dma((4 + NF,)), dma, dma,
            dma, dma((NT,)), dma, dma((NT,)), dma, dma((NF,)),
        ] + [dma, dma((slabs,))] * 6,
        compiler_params=pltpu.CompilerParams(
            collective_id=0, has_side_effects=True, vmem_limit_bytes=62 * 1024 * 1024
        ),
    )(*flat, conv_weight, proj_weight)
    raw = raw.reshape(slabs, 2, 3, CH, 128)
    grad_proj = raw[0].transpose(2, 1, 0, 3).reshape(FULL, CH)
    grad_conv = raw[1:].transpose(2, 3, 0, 1, 4).reshape(3, CH, FULL)
    return (grad_inputs.reshape(inputs.shape), grad_conv, grad_proj)


def solution(mesh):
    in_specs = (
        P(None, "seq", "ch"),
        P(None, "seq", "ch"),
        P(None, "seq", None),
        P(None, "ch", None),
        P(None, "ch"),
    )
    out_specs = (P(None, "seq", "ch"), P(None, "ch", None), P(None, "ch"))
    return jax.shard_map(shards, mesh=mesh, in_specs=in_specs, out_specs=out_specs, check_vma=False)
```

time: 703 us -> 225 us (0.32)
  blocking collectives: 518 us -> 0 us
  Pallas kernels: 0 us -> 204 us
  waiting for transfers between devices: 112 us -> 0 us
  matrix products: 46.7 us -> 0 us
  local copies, waits for them, and re-layouts: 1.63 us -> 19.8 us
  other arithmetic: 8.96 us -> 0 us
  starting transfers between devices: 7.37 us -> 0 us
    psum x2 -> x0, blocking collectives: 518 us -> none  [the longest x1 371 us: shards(): conv_total, proj_total = lax.psum((conv_terms, proj_terms), 'seq')]
    pallas_call x0 -> x1, Pallas kernels: none -> 204 us  [shards(): pl.pallas_call(kernel, out_shape=(jax.ShapeDtypeStruct((ROWS, CH), BF), j...]
    ppermute x2 -> x0, waiting for transfers between devices: 112 us -> none  [shifted(): lax.ppermute(value, axis, [(source, source + steps) for source in range(l...]
    dot_general x8 -> x0, matrix products: 46.7 us -> none  [the longest x3 24.8 us: shards(): jnp.dot(tap_list[tap_index], conv_weight[tap_index].T, preferred_element_...]
    ppermute x2 -> x0, starting transfers between devices: 7.37 us -> none  [shifted(): lax.ppermute(value, axis, [(source, source + steps) for source in range(l...]
  transfers between devices with their start and end apart: 2 -> 0, of which waited for: 1 -> 0; matrix products, arithmetic and copies ran while one was open for 4% -> 0% of each run, Pallas kernels for 0% -> 0%
where the time goes in v1:
time: 225 us
  Pallas kernels  204 us (91%)
  local copies, waits for them, and re-layouts  19.8 us (9%)
    pallas_call x1, Pallas kernels, shards(): pl.pallas_call(kernel, out_shape=(jax.ShapeDtypeStruct((ROWS, CH), BF), j...  204 us

profile of v1, /device:TPU:1, one launch (start us, length us, event | category | flops | bytes accessed | tf_op | source)
XLA Modules:
  0.0 224.8 jit_solution(15832176549654952768)
XLA Ops:
  0.6 204.3 %shard_map.76 = (bf16[2048,768]{1,0:T(8,128)(2,1)}, bf16[4,2,4,8,72,128]{5,4,3,2,1,0:T(8,128)(2,1)}) custom-call(bf16[2048,768]{1,0:T(8,128)(2,1)} %bitcast.12, bf16[2048,768]{1,0:T(8,128)(2,1)} %bitcast.13, bf16[2048,768]{1,0:T(8,128)(2,1)} %bitcast.14, bf16[3,768,768]{2,1,0:T(8,128)(2,1)} %cw_h.1, bf16[768,768]{1,0:T(8,128)(2,1)} %pw_h.1), custom_call_target="tpu_custom_call" | custom-call | tf_op jit(solution)/shard_map/pallas_call | solution.py:452
  204.9 2.4 %slice.12 = bf16[1,2,4,8,72,128]{5,4,3,2,1,0:T(8,128)(2,1)} slice(bf16[4,2,4,8,72,128]{5,4,3,2,1,0:T(8,128)(2,1)} %get-tuple-element.6), slice={[0:1], [0:2], [0:4], [0:8], [0:72], [0:128]} | slice | bytes 2359296 | tf_op jit(solution)/shard_map/slice | solution.py:477
  207.3 2.6 %slice.10 = bf16[3,2,4,8,72,128]{5,4,3,2,1,0:T(8,128)(2,1)S(1)} slice(bf16[4,2,4,8,72,128]{5,4,3,2,1,0:T(8,128)(2,1)} %get-tuple-element.6), slice={[1:4], [0:2], [0:4], [0:8], [0:72], [0:128]} | slice | bytes 7077888 | tf_op jit(solution)/shard_map/slice | solution.py:478
  210.0 3.6 %copy.8 = bf16[3,768,3,2,128]{4,3,2,1,0:T(2,128)(2,1)S(1)} copy(bf16[3,768,3,2,128]{4,1,0,3,2:T(8,128)(2,1)S(1)} %bitcast.10) | data formatting | bytes 7077888 | tf_op jit(solution)/shard_map/transpose | solution.py:478
  213.6 3.6 %reshape.32 = bf16[3,768,768]{2,1,0:T(8,128)(2,1)} reshape(bf16[3,768,3,2,128]{4,3,2,1,0:T(2,128)(2,1)S(1)} %copy.8) | data formatting | bytes 7077888 | tf_op jit(solution)/shard_map/reshape | solution.py:478
  217.2 2.5 %copy.9 = bf16[768,3,2,128]{3,2,1,0:T(2,128)(2,1)S(1)} copy(bf16[768,3,2,128]{3,0,1,2:T(8,128)(2,1)} %bitcast.11) | data formatting | bytes 2359296 | tf_op jit(solution)/shard_map/transpose | solution.py:477
  219.7 1.4 reshape.33
  221.0 3.8 %copy.11 = bf16[2,1024,768]{2,1,0:T(8,128)(2,1)} copy(bf16[2,1024,768]{2,1,0:T(8,128)(2,1)} %bitcast.15) | data formatting | bytes 6291456

commit v2 on v1

--- a/solution.py
+++ b/solution.py
@@ -20,8 +20,10 @@
 WINDOW = 6
 LAG = 2
 SLAB = 3 * CH
+ZH = SLAB // 2
 ZP = SLAB // 4
 XP = ZP // 8
+XS = XP // 3
 SCALE = 1.0 / math.sqrt(131072.0)
 BF = jnp.bfloat16
 F32 = jnp.float32
@@ -40,13 +42,13 @@
 
 
 def kernel(
-    inp_h, cot_h, cout_h, cw_h, pw_h, gi_h, wg_h,
+    inp_h, cot_h, cout_h, cw_h, pw_h, gi_h, gc_h, gp_h,
     cot, io, h_t, der, pw, cw, part, mid, mid_q, mid_x, gh,
-    slab, own32, z32, cs, cr, zs, zr, xs, xr, fin,
+    slab, z32, cs, cr, as_, ar, bs, br, xs, xr, fin,
     ld_sem, out_sem, wout_sem,
     e_send, e_recv, q_send, q_recv, x_send, x_recv,
-    c_send, c_recv, zz_send, zz_recv, xy_send, xy_recv,
-    axy_send, axy_recv, az_send, az_recv, ac_send, ac_recv,
+    c_send, c_recv, a_send, a_recv, b_send, b_recv, xy_send, xy_recv,
+    gx_send, gx_recv, gb_send, gb_recv, ga_send, ga_recv, gc_send, gc_recv,
 ):
     s = lax.axis_index("seq")
     c = lax.axis_index("ch")
@@ -66,11 +68,13 @@
     has_src = jnp.logical_and(behind >= 0, behind < 64)
     twin = dev(s + 1 - 2 * core, c)
 
-    def z_peer(d):
-        return (z + d) % 4
-
-    def z_dev(d):
-        return dev(z_peer(d) * 16 + s % 16, c)
+    next_z, mirror_z = z + 1 - 2 * (z % 2), 3 - z
+    dev_a = dev((next_z + core * (mirror_z - next_z)) * 16 + s % 16, c)
+    dev_b = dev((mirror_z + core * (next_z - mirror_z)) * 16 + s % 16, c)
+    upper, middle = z // 2, ((z + 1) // 2) % 2
+    half = middle + core * (upper - middle)
+    quarter = 2 * half + upper + core * (z % 2 - upper)
+    other_quarter = 4 * half + 1 - quarter
 
     def p_peer(d):
         return (p + d) % 8
@@ -100,8 +104,8 @@
     greet(partner)
     greet(across)
     greet(twin)
-    for d in range(1, 4):
-        greet(z_dev(d))
+    greet(dev_a)
+    greet(dev_b)
     for d in range(1, 8):
         greet(p_dev(d))
 
@@ -116,7 +120,7 @@
     def _():
         greet(dev(behind, c))
 
-    pl.semaphore_wait(barrier, 13 + far_dst.astype(jnp.int32) + far_src.astype(jnp.int32))
+    pl.semaphore_wait(barrier, 12 + far_dst.astype(jnp.int32) + far_src.astype(jnp.int32))
 
     def block(ref, t):
         return ref.at[t // NB, pl.ds(pl.multiple_of((t % NB) * RB, RB), RB)]
@@ -162,15 +166,16 @@
 
         return lax.fori_loop(0, NB, part_block, 0)
 
-    lax.fori_loop(0, NF, part_chunk, 0)
-
-    @pl.when(jnp.logical_not(has_src))
-    def _():
-        def clear(i, _):
-            mid_x[i // 32, pl.ds(pl.multiple_of((i % 32) * 64, 64), 64), :] = jnp.zeros((64, FW), BF)
-            return 0
-
-        lax.fori_loop(0, 32 * NF, clear, 0)
+    part_chunk(0, 0)
+
+    def clear_x():
+        @pl.when(jnp.logical_not(has_src))
+        def _():
+            def clear(i, _):
+                mid_x[i // 32, pl.ds(pl.multiple_of((i % 32) * 64, 64), 64), :] = jnp.zeros((64, FW), BF)
+                return 0
+
+            lax.fori_loop(0, 32 * NF, clear, 0)
 
     def service(t):
         wait_for(block(mid, t), e_recv.at[t])
@@ -190,112 +195,119 @@
         lax.fori_loop(0, RB // 64, add, 0)
         start_q(t)
 
-    def store_slab(row, value):
-        rows = pl.ds(pl.multiple_of(row, 256), 256)
-        slab[0, rows, :] = value[:, :128]
-        slab[1, rows, :] = value[:, 128:]
-
-    ld_cout.wait()
-
-    def turn(i, _):
-        span = pl.ds(pl.multiple_of(i * 128, 128), 128)
-        h_t[:, span] = io[span, :].T
-        return 0
-
-    lax.fori_loop(0, ROWS // 128, turn, 0)
-    ld_inp.start()
-    for k in range(3):
-        def proj_tile(i, _, k=k):
-            rows = pl.ds(pl.multiple_of(i * 256, 256), 256)
-            store_slab(k * CH + i * 256, dot(h_t[rows, :], cot[:, k * 256:(k + 1) * 256]))
-            return 0
-
-        lax.fori_loop(0, 3, proj_tile, 0)
+    def turn_rows():
+        def turn(i, _):
+            span = pl.ds(pl.multiple_of(i * 128, 128), 128)
+            h_t[:, span] = io[span, :].T
+            return 0
+
+        lax.fori_loop(0, ROWS // 128, turn, 0)
+
+    def proj_block(k):
+        def proj_tile(i, _):
+            rows = pl.ds(pl.multiple_of(i * 384, 384), 384)
+            value = dot(h_t[rows, :], cot[:, k * 256:(k + 1) * 256])
+            for j in range(384 // XS):
+                spot = pl.ds(pl.multiple_of((i * (384 // XS) + j) * XP + k * XS, 8), XS)
+                slab[0, 0, spot, :] = value[j * XS:(j + 1) * XS, :128]
+                slab[0, 1, spot, :] = value[j * XS:(j + 1) * XS, 128:]
+            return 0
+
+        lax.fori_loop(0, 2, proj_tile, 0)
+
+    def send(src, dst, send_sem, recv_sem, device):
+        pltpu.make_async_remote_copy(
+            src_ref=src, dst_ref=dst, send_sem=send_sem, recv_sem=recv_sem, device_id=device, device_id_type=MESH
+        ).start()
 
     def core_send(g):
         def cast(i, _):
-            rows = pl.ds(pl.multiple_of(i * 64, 64), 64)
-            cs[g, rows, :] = slab[1 - core, rows, :].astype(BF)
-            return 0
-
-        lax.fori_loop(0, SLAB // 64, cast, 0)
-        pltpu.make_async_remote_copy(
-            src_ref=cs.at[g], dst_ref=cr.at[g], send_sem=c_send, recv_sem=c_recv.at[g],
-            device_id=twin, device_id_type=MESH,
-        ).start()
-
-    def z_send(g):
+            rows = pl.ds(pl.multiple_of(i * 128, 128), 128)
+            cs[g, rows, :] = slab[g % 2, 1 - core, rows, :].astype(BF)
+            return 0
+
+        lax.fori_loop(0, SLAB // 128, cast, 0)
+        send(cs.at[g], cr.at[g], c_send, c_recv.at[g], twin)
+
+    def a_exchange(g):
         wait_for(cr.at[g], c_recv.at[g])
+
+        def add(i, _):
+            rows = pl.ds(pl.multiple_of((1 - half) * ZH + i * 128, 128), 128)
+            total = slab[g % 2, core, rows, :] + cr[g, rows, :].astype(F32)
+            as_[g, pl.ds(pl.multiple_of(i * 128, 128), 128), :] = total.astype(BF)
+            return 0
+
+        lax.fori_loop(0, ZH // 128, add, 0)
+        send(as_.at[g], ar.at[g], a_send, a_recv.at[g], dev_a)
+
+    def quarter_sum(g, which, i):
+        rows = pl.ds(pl.multiple_of(which * ZP + i * 64, 64), 64)
+        inner = pl.ds(pl.multiple_of((which - 2 * half) * ZP + i * 64, 64), 64)
+        return slab[g % 2, core, rows, :] + cr[g, rows, :].astype(F32) + ar[g, inner, :].astype(F32)
+
+    def b_exchange(g):
+        wait_for(ar.at[g], a_recv.at[g])
+
+        def add(i, _):
+            bs[g, pl.ds(pl.multiple_of(i * 64, 64), 64), :] = quarter_sum(g, other_quarter, i).astype(BF)
+            return 0
+
+        lax.fori_loop(0, ZP // 64, add, 0)
+        send(bs.at[g], br.at[g], b_send, b_recv.at[g], dev_b)
+
+    def x_exchange(g):
+        wait_for(br.at[g], b_recv.at[g])
 
         def add(i, _):
             rows = pl.ds(pl.multiple_of(i * 64, 64), 64)
-            total = slab[core, rows, :] + cr[g, rows, :].astype(F32)
-            slab[core, rows, :] = total
-            zs[g, i // (ZP // 64), pl.ds(pl.multiple_of((i % (ZP // 64)) * 64, 64), 64), :] = total.astype(BF)
-            return 0
-
-        lax.fori_loop(0, SLAB // 64, add, 0)
-        own32[...] = slab[core, pl.ds(pl.multiple_of(z * ZP, 64), ZP), :]
-        for d in range(1, 4):
-            pltpu.make_async_remote_copy(
-                src_ref=zs.at[g, z_peer(d)], dst_ref=zr.at[g, d - 1], send_sem=zz_send, recv_sem=zz_recv.at[g],
-                device_id=z_dev(d), device_id_type=MESH,
-            ).start()
-
-    def x_send_sum(g):
-        wait_for(zr.at[g], zz_recv.at[g])
-
-        def add(i, _):
-            rows = pl.ds(pl.multiple_of(i * 64, 64), 64)
-            z32[rows, :] = (own32[rows, :] + zr[g, 0, rows, :].astype(F32)) + (
-                zr[g, 1, rows, :].astype(F32) + zr[g, 2, rows, :].astype(F32)
-            )
+            z32[rows, :] = quarter_sum(g, quarter, i) + br[g, rows, :].astype(F32)
             return 0
 
         lax.fori_loop(0, ZP // 64, add, 0)
         for i in range(8):
             xs[g, i] = z32[i * XP:(i + 1) * XP, :].astype(BF)
         for d in range(1, 8):
-            pltpu.make_async_remote_copy(
-                src_ref=xs.at[g, p_peer(d)], dst_ref=xr.at[g, d - 1], send_sem=xy_send, recv_sem=xy_recv.at[g],
-                device_id=p_dev(d), device_id_type=MESH,
-            ).start()
+            send(xs.at[g, p_peer(d)], xr.at[g, d - 1], xy_send, xy_recv.at[g], p_dev(d))
 
     def finish(g):
         wait_for(xr.at[g], xy_recv.at[g])
         total = z32[pl.ds(pl.multiple_of(p * XP, 8), XP), :]
         for d in range(7):
             total = total + xr[g, d].astype(F32)
-        fin[g, core, z, p] = (total * SCALE).astype(BF)
+        fin[g, core, quarter * 8 + p] = (total * SCALE).astype(BF)
+        piece = fin.at[g, core, quarter * 8 + p]
         for d in range(1, 8):
-            piece = fin.at[g, core, z, p]
-            pltpu.make_async_remote_copy(
-                src_ref=piece, dst_ref=piece, send_sem=axy_send, recv_sem=axy_recv.at[g],
-                device_id=p_dev(d), device_id_type=MESH,
-            ).start()
-
-    def gather_z(g):
-        wait_for(xr.at[g], axy_recv.at[g])
-        for d in range(1, 4):
-            piece = fin.at[g, core, z]
-            pltpu.make_async_remote_copy(
-                src_ref=piece, dst_ref=piece, send_sem=az_send, recv_sem=az_recv.at[g],
-                device_id=z_dev(d), device_id_type=MESH,
-            ).start()
+            send(piece, piece, gx_send, gx_recv.at[g], p_dev(d))
+
+    def gather_b(g):
+        wait_for(xr.at[g], gx_recv.at[g])
+        piece = fin.at[g, core, pl.ds(quarter * 8, 8)]
+        send(piece, piece, gb_send, gb_recv.at[g], dev_b)
+
+    def gather_a(g):
+        wait_for(fin.at[g, core, pl.ds(0, 8)], gb_recv.at[g])
+        piece = fin.at[g, core, pl.ds(half * 16, 16)]
+        send(piece, piece, ga_send, ga_recv.at[g], dev_a)
 
     def gather_core(g):
-        wait_for(fin.at[g, core, pl.ds(0, 3)], az_recv.at[g])
+        wait_for(fin.at[g, core, pl.ds(0, 16)], ga_recv.at[g])
         piece = fin.at[g, core]
-        pltpu.make_async_remote_copy(
-            src_ref=piece, dst_ref=piece, send_sem=ac_send, recv_sem=ac_recv.at[g],
-            device_id=twin, device_id_type=MESH,
-        ).start()
+        send(piece, piece, gc_send, gc_recv.at[g], twin)
 
     def write_out(g):
-        wait_for(fin.at[g, 1 - core], ac_recv.at[g])
-        pltpu.make_async_copy(fin.at[g], wg_h.at[g], wout_sem).start()
-
-    core_send(0)
+        wait_for(fin.at[g, 1 - core], gc_recv.at[g])
+        for h in range(2):
+            if g == 0:
+                for k in range(3):
+                    pltpu.make_async_copy(
+                        fin.at[0, h, :, pl.ds(k * XS, XS), :],
+                        gp_h.at[:, :, pl.ds(k * FW + h * 128, 128)], wout_sem,
+                    ).start()
+            else:
+                pltpu.make_async_copy(
+                    fin.at[g, h], gc_h.at[:, :, pl.ds((g - 1) * FW + h * 128, 128)], wout_sem
+                ).start()
 
     def gelu(i):
         def tile(j, _):
@@ -316,18 +328,37 @@
 
         lax.fori_loop(0, RB // 128, tile, 0)
 
-    ld_inp.wait()
     for i in range(NB):
         service(i)
         if i >= LAG:
             forward_x(i - LAG)
-        if i == 2:
-            z_send(0)
-        if i == 4:
-            x_send_sum(0)
-        if i == 6:
-            finish(0)
-        gelu(i)
+        if i == 0:
+            part_chunk(1, 0)
+        elif i == 1:
+            ld_cout.wait()
+            turn_rows()
+            ld_inp.start()
+            clear_x()
+        elif i == 2:
+            proj_block(0)
+            proj_block(1)
+        elif i == 3:
+            proj_block(2)
+            core_send(0)
+        elif i == 4:
+            part_chunk(2, 0)
+        elif i == 5:
+            ld_inp.wait()
+            gelu(0)
+            a_exchange(0)
+            gelu(1)
+        elif i == 6:
+            for r in (2, 3, 4):
+                gelu(r)
+        else:
+            b_exchange(0)
+            for r in (5, 6, 7):
+                gelu(r)
 
     for cp in ld_cw:
         cp.wait()
@@ -338,7 +369,10 @@
     def weight_tap(f, tap, taps):
         def tile(i, _):
             rows = pl.ds(pl.multiple_of(i * 256, 256), 256)
-            store_slab(tap * CH + i * 256, dot(h_t[rows, :], taps[f]))
+            value = dot(h_t[rows, :], taps[f])
+            spot = pl.ds(pl.multiple_of(tap * CH + i * 256, 256), 256)
+            slab[(f + 1) % 2, 0, spot, :] = value[:, :128]
+            slab[(f + 1) % 2, 1, spot, :] = value[:, 128:]
             return 0
 
         lax.fori_loop(0, CH // 256, tile, 0)
@@ -392,12 +426,21 @@
                     forward_x(t - LAG)
 
         serve(0)
-        gather_z(g - 1)
         weight_tap(f, 1, mid)
         serve(1)
+        x_exchange(g - 1)
         weight_tap(f, tap_q, mid_q)
         serve(2)
-        gather_core(g - 1)
+        finish(g - 1)
+
+        @pl.when(g == 2)
+        def _():
+            write_out(0)
+
+        @pl.when(g == 3)
+        def _():
+            write_out(1)
+
         serve(3)
 
         @pl.when(has_src)
@@ -407,20 +450,26 @@
         weight_tap(f, tap_x, mid_x)
         core_send(g)
         serve(4)
-        data_rows(g, 0, NB // 2)
+        gather_b(g - 1)
+        data_rows(g, 0, 2)
         serve(5)
-        z_send(g)
-        write_out(g - 1)
-        data_rows(g, NB // 2, NB // 4)
+        a_exchange(g)
+        data_rows(g, 2, 2)
         serve(6)
-        x_send_sum(g)
-        data_rows(g, NB // 2 + NB // 4, NB // 4)
+        gather_a(g - 1)
+        data_rows(g, 4, 2)
         serve(7)
-        finish(g)
+        b_exchange(g)
+        gather_core(g - 1)
+        data_rows(g, 6, 2)
         return 0
 
     lax.fori_loop(1, NF + 1, phase, 0)
-    gather_z(NF)
+    x_exchange(NF)
+    finish(NF)
+    write_out(NF - 1)
+    gather_b(NF)
+    gather_a(NF)
     gather_core(NF)
     write_out(NF)
 
@@ -432,12 +481,14 @@
         wait_for(mid_q, x_send)
 
     wait_for(cs, c_send)
-    wait_for(zr, zz_send)
+    wait_for(as_, a_send)
+    wait_for(bs, b_send)
     wait_for(xr, xy_send)
-    wait_for(xr, axy_send)
+    wait_for(xr, gx_send)
     for g in range(NF + 1):
-        wait_for(fin.at[g, 0, pl.ds(0, 3)], az_send)
-        wait_for(fin.at[g, 0], ac_send)
+        wait_for(fin.at[g, 0, pl.ds(0, 8)], gb_send)
+        wait_for(fin.at[g, 0, pl.ds(0, 16)], ga_send)
+        wait_for(fin.at[g, 0], gc_send)
     wait_for(io, out_sem)
     wait_for(fin, wout_sem)
 
@@ -449,33 +500,34 @@
     rows_bf = pltpu.VMEM((ROWS, CH), BF)
     chunks = pltpu.VMEM((NF, ROWS, FW), BF)
     flat = [a.reshape(ROWS, CH) for a in (inputs, cotangent, conv_out)]
-    grad_inputs, raw = pl.pallas_call(
+    grad_inputs, grad_conv, grad_proj = pl.pallas_call(
         kernel,
         out_shape=(
             jax.ShapeDtypeStruct((ROWS, CH), BF),
-            jax.ShapeDtypeStruct((slabs, 2, 4, 8, XP, 128), BF),
+            jax.ShapeDtypeStruct((32, XP, FULL), BF),
+            jax.ShapeDtypeStruct((32, XS, CH), BF),
         ),
         in_specs=[any_spec] * 5,
-        out_specs=(any_spec, any_spec),
+        out_specs=(any_spec,) * 3,
         scratch_shapes=[
             rows_bf, rows_bf, pltpu.VMEM((CH, ROWS), BF), pltpu.VMEM((ROWS, CH), F32),
             pltpu.VMEM((FULL, CH), BF), pltpu.VMEM((NF, 3, CH, FW), BF),
             chunks, chunks, chunks, chunks, pltpu.VMEM((ROWS, CH), F32),
-            pltpu.VMEM((2, SLAB, 128), F32), pltpu.VMEM((ZP, 128), F32), pltpu.VMEM((ZP, 128), F32),
+            pltpu.VMEM((2, 2, SLAB, 128), F32), pltpu.VMEM((ZP, 128), F32),
             pltpu.VMEM((slabs, SLAB, 128), BF), pltpu.VMEM((slabs, SLAB, 128), BF),
-            pltpu.VMEM((slabs, 4, ZP, 128), BF), pltpu.VMEM((slabs, 3, ZP, 128), BF),
+            pltpu.VMEM((slabs, ZH, 128), BF), pltpu.VMEM((slabs, ZH, 128), BF),
+            pltpu.VMEM((slabs, ZP, 128), BF), pltpu.VMEM((slabs, ZP, 128), BF),
             pltpu.VMEM((slabs, 8, XP, 128), BF), pltpu.VMEM((slabs, 7, XP, 128), BF),
-            pltpu.VMEM((slabs, 2, 4, 8, XP, 128), BF),
+            pltpu.VMEM((slabs, 2, 32, XP, 128), BF),
             dma((4 + NF,)), dma, dma,
             dma, dma((NT,)), dma, dma((NT,)), dma, dma((NF,)),
-        ] + [dma, dma((slabs,))] * 6,
+        ] + [dma, dma((slabs,))] * 8,
         compiler_params=pltpu.CompilerParams(
             collective_id=0, has_side_effects=True, vmem_limit_bytes=62 * 1024 * 1024
         ),
     )(*flat, conv_weight, proj_weight)
-    raw = raw.reshape(slabs, 2, 3, CH, 128)
-    grad_proj = raw[0].transpose(2, 1, 0, 3).reshape(FULL, CH)
-    grad_conv = raw[1:].transpose(2, 3, 0, 1, 4).reshape(3, CH, FULL)
+    grad_conv = grad_conv.reshape(3, CH, FULL)
+    grad_proj = grad_proj.reshape(FULL, CH)
     return (grad_inputs.reshape(inputs.shape), grad_conv, grad_proj)
 
 

time: 225 us -> 192 us (0.85)
  Pallas kernels: 204 us -> 184 us
  local copies, waits for them, and re-layouts: 19.8 us -> 7.02 us
    pallas_call x1, Pallas kernels: 204 us -> 184 us  [shards(): pl.pallas_call(kernel, out_shape=(jax.ShapeDtypeStruct((ROWS, CH), BF), j...]
    transpose x2 -> x0, local copies, waits for them, and re-layouts: 6.12 us -> none  [the longest x1 3.64 us: shards(): grad_conv = raw[1:].transpose(2, 3, 0, 1, 4).reshape(3, CH, FULL)]
    slice x2 -> x0, local copies, waits for them, and re-layouts: 5.01 us -> none  [the longest x1 2.63 us: shards(): grad_conv = raw[1:].transpose(2, 3, 0, 1, 4).reshape(3, CH, FULL)]
    reshape x2 -> x0, local copies, waits for them, and re-layouts: 4.95 us -> none  [the longest x1 3.56 us: shards(): grad_conv = raw[1:].transpose(2, 3, 0, 1, 4).reshape(3, CH, FULL)]
    unnamed x1 -> x7, local copies, waits for them, and re-layouts: 3.75 us -> 7.02 us
where the time goes in v2:
time: 192 us; the launch traced here: 191 us
  Pallas kernels  184 us (96%)
  local copies, waits for them, and re-layouts  7.02 us (4%)
    pallas_call x1, Pallas kernels, shards(): pl.pallas_call(kernel, out_shape=(jax.ShapeDtypeStruct((ROWS, CH), BF), j...  184 us
    unnamed x7, local copies, waits for them, and re-layouts  7.02 us

profile of v2, /device:TPU:1, one launch (start us, length us, event | category | flops | bytes accessed | tf_op | source)
XLA Modules:
  0.0 191.3 jit_solution(16792478391429849058)
XLA Ops:
  0.6 183.6 %shard_map.76 = (bf16[2048,768]{1,0:T(8,128)(2,1)}, bf16[32,72,768]{2,1,0:T(8,128)(2,1)}, bf16[32,24,768]{2,1,0:T(8,128)(2,1)}) custom-call(bf16[2048,768]{1,0:T(8,128)(2,1)} %bitcast.7, bf16[2048,768]{1,0:T(8,128)(2,1)} %bitcast.8, bf16[2048,768]{1,0:T(8,128)(2,1)} %bitcast.9, bf16[3,768,768]{2,1,0:T(8,128)(2,1)} %cw_h.1, bf16[768,768]{1,0:T(8,128)(2,1)} %pw_h.1), custom_call_target="tpu_custom_call" | custom-call | tf_op jit(solution)/shard_map/pallas_call | solution.py:503
  184.3 0.0 copy-start
  184.3 3.9 %copy.11 = bf16[2,1024,768]{2,1,0:T(8,128)(2,1)} copy(bf16[2,1024,768]{2,1,0:T(8,128)(2,1)} %bitcast.10) | data formatting | bytes 6291456
  188.2 0.0 copy-done
  188.2 0.0 copy-start.1
  188.2 1.8 copy.12
  190.0 0.3 copy-done.1
  190.3 1.0 copy.13
Async XLA Ops:
  184.3 3.9 %copy-start = (bf16[32,72,768]{2,1,0:T(8,128)(2,1)S(1)}, bf16[32,72,768]{2,1,0:T(8,128)(2,1)}, u32[]{:S(2)}) copy-start(bf16[32,72,768]{2,1,0:T(8,128)(2,1)} %get-tuple-element.7) | copy-start | bytes 10616836
  188.2 2.1 %copy-start.1 = (bf16[32,24,768]{2,1,0:T(8,128)(2,1)S(1)}, bf16[32,24,768]{2,1,0:T(8,128)(2,1)}, u32[]{:S(2)}) copy-start(bf16[32,24,768]{2,1,0:T(8,128)(2,1)} %get-tuple-element.8) | copy-start | bytes 3538948

commit v3 on v2

--- a/solution.py
+++ b/solution.py
@@ -19,6 +19,14 @@
 NT = NF * NB
 WINDOW = 6
 LAG = 2
+X_TICK = 5
+TICKS = (
+    (3, 5, 22, 24, 25, 26, 27, 28, 29, 30),
+    (13, 15, 22, 24, 25, 26, 27, 28, 29, 30),
+    (21, 23, 24, 25, 26, 27, 28, 29, 30, 31),
+    (27, 28, 28, 29, 30, 31, 32, 33, 34, 35),
+)
+AXES = (0, 1, 0, 1)
 SLAB = 3 * CH
 ZH = SLAB // 2
 ZP = SLAB // 4
@@ -44,7 +52,7 @@
 def kernel(
     inp_h, cot_h, cout_h, cw_h, pw_h, gi_h, gc_h, gp_h,
     cot, io, h_t, der, pw, cw, part, mid, mid_q, mid_x, gh,
-    slab, z32, cs, cr, as_, ar, bs, br, xs, xr, fin,
+    slab, keep, z32, cs, cr, as_, ar, bs, br, xs, xr, fin,
     ld_sem, out_sem, wout_sem,
     e_send, e_recv, q_send, q_recv, x_send, x_recv,
     c_send, c_recv, a_send, a_recv, b_send, b_recv, xy_send, xy_recv,
@@ -54,7 +62,6 @@
     c = lax.axis_index("ch")
     core = s % 2
     yh = (s // 2) % 2
-    p = (s // 2) % 8
     z = s // 16
 
     def dev(seq, ch):
@@ -68,19 +75,31 @@
     has_src = jnp.logical_and(behind >= 0, behind < 64)
     twin = dev(s + 1 - 2 * core, c)
 
-    next_z, mirror_z = z + 1 - 2 * (z % 2), 3 - z
-    dev_a = dev((next_z + core * (mirror_z - next_z)) * 16 + s % 16, c)
-    dev_b = dev((mirror_z + core * (next_z - mirror_z)) * 16 + s % 16, c)
-    upper, middle = z // 2, ((z + 1) // 2) % 2
-    half = middle + core * (upper - middle)
-    quarter = 2 * half + upper + core * (z % 2 - upper)
-    other_quarter = 4 * half + 1 - quarter
-
-    def p_peer(d):
-        return (p + d) % 8
-
-    def p_dev(d):
-        return dev(z * 16 + p_peer(d) * 2 + core, c)
+    x = (s // 4) % 4
+
+    def geometry(i, j, axis):
+        def at_axis(k):
+            return dev(k * 16 + s % 16 if axis == 0 else z * 16 + k * 4 + s % 4, c)
+
+        following, mirror = i + 1 - 2 * (i % 2), 3 - i
+        upper, middle = i // 2, ((i + 1) // 2) % 2
+        half = middle + core * (upper - middle)
+        quarter = 2 * half + upper + core * (i % 2 - upper)
+        place = j * 2 + yh
+
+        def peer(d):
+            return (place + d) % 8
+
+        def peer_dev(d):
+            jj, yy = peer(d) // 2, peer(d) % 2
+            return dev(z * 16 + jj * 4 + yy * 2 + core if axis == 0 else jj * 16 + x * 4 + yy * 2 + core, c)
+
+        return dict(
+            dev_a=at_axis(following + core * (mirror - following)), dev_b=at_axis(mirror + core * (following - mirror)),
+            half=half, quarter=quarter, other=4 * half + 1 - quarter, place=place, peer=peer, peer_dev=peer_dev,
+        )
+
+    geometries = (geometry(z, x, 0), geometry(x, z, 1))
 
     ld_cot = pltpu.make_async_copy(cot_h, cot, ld_sem.at[0])
     ld_pw = pltpu.make_async_copy(pw_h, pw, ld_sem.at[1])
@@ -104,10 +123,11 @@
     greet(partner)
     greet(across)
     greet(twin)
-    greet(dev_a)
-    greet(dev_b)
     for d in range(1, 8):
-        greet(p_dev(d))
+        greet(geometries[0]["peer_dev"](d))
+    for d in range(1, 4):
+        for other_yh in range(2):
+            greet(dev(((z + d) % 4) * 16 + x * 4 + other_yh * 2 + core, c))
 
     far_dst = jnp.logical_and(has_dst, ahead // 16 != z)
     far_src = jnp.logical_and(has_src, behind // 16 != z)
@@ -120,7 +140,7 @@
     def _():
         greet(dev(behind, c))
 
-    pl.semaphore_wait(barrier, 12 + far_dst.astype(jnp.int32) + far_src.astype(jnp.int32))
+    pl.semaphore_wait(barrier, 16 + far_dst.astype(jnp.int32) + far_src.astype(jnp.int32))
 
     def block(ref, t):
         return ref.at[t // NB, pl.ds(pl.multiple_of((t % NB) * RB, RB), RB)]
@@ -209,8 +229,8 @@
             value = dot(h_t[rows, :], cot[:, k * 256:(k + 1) * 256])
             for j in range(384 // XS):
                 spot = pl.ds(pl.multiple_of((i * (384 // XS) + j) * XP + k * XS, 8), XS)
-                slab[0, 0, spot, :] = value[j * XS:(j + 1) * XS, :128]
-                slab[0, 1, spot, :] = value[j * XS:(j + 1) * XS, 128:]
+                slab[0, spot, :] = value[j * XS:(j + 1) * XS, :128]
+                slab[1, spot, :] = value[j * XS:(j + 1) * XS, 128:]
             return 0
 
         lax.fori_loop(0, 2, proj_tile, 0)
@@ -223,72 +243,82 @@
     def core_send(g):
         def cast(i, _):
             rows = pl.ds(pl.multiple_of(i * 128, 128), 128)
-            cs[g, rows, :] = slab[g % 2, 1 - core, rows, :].astype(BF)
+            cs[g, rows, :] = slab[1 - core, rows, :].astype(BF)
             return 0
 
         lax.fori_loop(0, SLAB // 128, cast, 0)
         send(cs.at[g], cr.at[g], c_send, c_recv.at[g], twin)
 
+    def core_sum(g):
+        half = geometries[AXES[g]]["half"]
+        wait_for(cr.at[g], c_recv.at[g])
+
+        def add(i, _):
+            inner = pl.ds(pl.multiple_of(i * 128, 128), 128)
+            mine = pl.ds(pl.multiple_of(half * ZH + i * 128, 128), 128)
+            other = pl.ds(pl.multiple_of((1 - half) * ZH + i * 128, 128), 128)
+            keep[g, inner, :] = slab[core, mine, :] + cr[g, mine, :].astype(F32)
+            as_[g, inner, :] = (slab[core, other, :] + cr[g, other, :].astype(F32)).astype(BF)
+            return 0
+
+        lax.fori_loop(0, ZH // 128, add, 0)
+
     def a_exchange(g):
-        wait_for(cr.at[g], c_recv.at[g])
-
-        def add(i, _):
-            rows = pl.ds(pl.multiple_of((1 - half) * ZH + i * 128, 128), 128)
-            total = slab[g % 2, core, rows, :] + cr[g, rows, :].astype(F32)
-            as_[g, pl.ds(pl.multiple_of(i * 128, 128), 128), :] = total.astype(BF)
-            return 0
-
-        lax.fori_loop(0, ZH // 128, add, 0)
-        send(as_.at[g], ar.at[g], a_send, a_recv.at[g], dev_a)
+        send(as_.at[g], ar.at[g], a_send, a_recv.at[g], geometries[AXES[g]]["dev_a"])
 
     def quarter_sum(g, which, i):
-        rows = pl.ds(pl.multiple_of(which * ZP + i * 64, 64), 64)
+        half = geometries[AXES[g]]["half"]
         inner = pl.ds(pl.multiple_of((which - 2 * half) * ZP + i * 64, 64), 64)
-        return slab[g % 2, core, rows, :] + cr[g, rows, :].astype(F32) + ar[g, inner, :].astype(F32)
+        return keep[g, inner, :] + ar[g, inner, :].astype(F32)
 
     def b_exchange(g):
         wait_for(ar.at[g], a_recv.at[g])
 
         def add(i, _):
-            bs[g, pl.ds(pl.multiple_of(i * 64, 64), 64), :] = quarter_sum(g, other_quarter, i).astype(BF)
+            total = quarter_sum(g, geometries[AXES[g]]["other"], i)
+            bs[g, pl.ds(pl.multiple_of(i * 64, 64), 64), :] = total.astype(BF)
             return 0
 
         lax.fori_loop(0, ZP // 64, add, 0)
-        send(bs.at[g], br.at[g], b_send, b_recv.at[g], dev_b)
+        send(bs.at[g], br.at[g], b_send, b_recv.at[g], geometries[AXES[g]]["dev_b"])
 
     def x_exchange(g):
+        geo = geometries[AXES[g]]
         wait_for(br.at[g], b_recv.at[g])
 
         def add(i, _):
             rows = pl.ds(pl.multiple_of(i * 64, 64), 64)
-            z32[rows, :] = quarter_sum(g, quarter, i) + br[g, rows, :].astype(F32)
+            z32[g, rows, :] = quarter_sum(g, geo["quarter"], i) + br[g, rows, :].astype(F32)
             return 0
 
         lax.fori_loop(0, ZP // 64, add, 0)
         for i in range(8):
-            xs[g, i] = z32[i * XP:(i + 1) * XP, :].astype(BF)
+            xs[g, i] = z32[g, i * XP:(i + 1) * XP, :].astype(BF)
         for d in range(1, 8):
-            send(xs.at[g, p_peer(d)], xr.at[g, d - 1], xy_send, xy_recv.at[g], p_dev(d))
+            send(xs.at[g, geo["peer"](d)], xr.at[g, d - 1], xy_send, xy_recv.at[g], geo["peer_dev"](d))
 
     def finish(g):
+        geo = geometries[AXES[g]]
         wait_for(xr.at[g], xy_recv.at[g])
-        total = z32[pl.ds(pl.multiple_of(p * XP, 8), XP), :]
+        total = z32[g, pl.ds(pl.multiple_of(geo["place"] * XP, 8), XP), :]
         for d in range(7):
             total = total + xr[g, d].astype(F32)
-        fin[g, core, quarter * 8 + p] = (total * SCALE).astype(BF)
-        piece = fin.at[g, core, quarter * 8 + p]
+        fin[g, core, geo["quarter"] * 8 + geo["place"]] = (total * SCALE).astype(BF)
+        piece = fin.at[g, core, geo["quarter"] * 8 + geo["place"]]
         for d in range(1, 8):
-            send(piece, piece, gx_send, gx_recv.at[g], p_dev(d))
+            send(piece, piece, gx_send, gx_recv.at[g], geo["peer_dev"](d))
 
     def gather_b(g):
+        geo = geometries[AXES[g]]
         wait_for(xr.at[g], gx_recv.at[g])
-        piece = fin.at[g, core, pl.ds(quarter * 8, 8)]
-        send(piece, piece, gb_send, gb_recv.at[g], dev_b)
+        piece = fin.at[g, core, pl.ds(geo["quarter"] * 8, 8)]
+        send(piece, piece, gb_send, gb_recv.at[g], geo["dev_b"])
 
     def gather_a(g):
+        geo = geometries[AXES[g]]
         wait_for(fin.at[g, core, pl.ds(0, 8)], gb_recv.at[g])
-        piece = fin.at[g, core, pl.ds(half * 16, 16)]
-        send(piece, piece, ga_send, ga_recv.at[g], dev_a)
+        piece = fin.at[g, core, pl.ds(geo["half"] * 16, 16)]
+        send(piece, piece, ga_send, ga_recv.at[g], geo["dev_a"])
 
     def gather_core(g):
         wait_for(fin.at[g, core, pl.ds(0, 16)], ga_recv.at[g])
@@ -328,41 +358,6 @@
 
         lax.fori_loop(0, RB // 128, tile, 0)
 
-    for i in range(NB):
-        service(i)
-        if i >= LAG:
-            forward_x(i - LAG)
-        if i == 0:
-            part_chunk(1, 0)
-        elif i == 1:
-            ld_cout.wait()
-            turn_rows()
-            ld_inp.start()
-            clear_x()
-        elif i == 2:
-            proj_block(0)
-            proj_block(1)
-        elif i == 3:
-            proj_block(2)
-            core_send(0)
-        elif i == 4:
-            part_chunk(2, 0)
-        elif i == 5:
-            ld_inp.wait()
-            gelu(0)
-            a_exchange(0)
-            gelu(1)
-        elif i == 6:
-            for r in (2, 3, 4):
-                gelu(r)
-        else:
-            b_exchange(0)
-            for r in (5, 6, 7):
-                gelu(r)
-
-    for cp in ld_cw:
-        cp.wait()
-
     tap_q = 2 * yh
     tap_x = 2 - 2 * yh
 
@@ -371,31 +366,20 @@
             rows = pl.ds(pl.multiple_of(i * 256, 256), 256)
             value = dot(h_t[rows, :], taps[f])
             spot = pl.ds(pl.multiple_of(tap * CH + i * 256, 256), 256)
-            slab[(f + 1) % 2, 0, spot, :] = value[:, :128]
-            slab[(f + 1) % 2, 1, spot, :] = value[:, 128:]
+            slab[0, spot, :] = value[:, :128]
+            slab[1, spot, :] = value[:, 128:]
             return 0
 
         lax.fori_loop(0, CH // 256, tile, 0)
 
-    def data_rows(g, first, count):
-        f = g - 1
-
+    def data_rows(f, first, count):
         def tile(i, _):
             rows = pl.ds(pl.multiple_of(i * RB, RB), RB)
             total = dot_t(mid[f, rows, :], cw[f, 1])
             total = total + dot_t(mid_q[f, rows, :], cw[f, tap_q])
             total = total + dot_t(mid_x[f, rows, :], cw[f, tap_x])
-
-            @pl.when(g == 1)
-            def _():
-                gh[rows, :] = total
-
-            @pl.when(g > 1)
-            def _():
-                gh[rows, :] = gh[rows, :] + total
-
-            @pl.when(g == NF)
-            def _():
+            gh[rows, :] = total if f == 0 else gh[rows, :] + total
+            if f == NF - 1:
                 def strip(m, _):
                     sub = pl.ds(pl.multiple_of(i * RB + m * 16, 16), 16)
                     io[sub, :] = (cot[sub, :].astype(F32) + gh[sub, :] * der[sub, :]).astype(BF)
@@ -403,75 +387,63 @@
 
                 lax.fori_loop(0, RB // 16, strip, 0)
                 pltpu.make_async_copy(io.at[rows], gi_h.at[rows], out_sem).start()
-
             return 0
 
         lax.fori_loop(first, first + count, tile, 0)
 
-    def phase(g, _):
-        f = g - 1
-
-        def serve(i):
-            t = g * NB + i
-
-            @pl.when(g < NF)
-            def _():
-                service(t)
-
-            if i < LAG:
-                forward_x(t - LAG)
-            else:
-                @pl.when(g < NF)
-                def _():
-                    forward_x(t - LAG)
-
-        serve(0)
-        weight_tap(f, 1, mid)
-        serve(1)
-        x_exchange(g - 1)
-        weight_tap(f, tap_q, mid_q)
-        serve(2)
-        finish(g - 1)
-
-        @pl.when(g == 2)
-        def _():
-            write_out(0)
-
-        @pl.when(g == 3)
-        def _():
-            write_out(1)
-
-        serve(3)
-
+    def x_tap(f):
         @pl.when(has_src)
         def _():
             wait_for(mid_x.at[f], x_recv.at[f])
 
         weight_tap(f, tap_x, mid_x)
-        core_send(g)
-        serve(4)
-        gather_b(g - 1)
-        data_rows(g, 0, 2)
-        serve(5)
-        a_exchange(g)
-        data_rows(g, 2, 2)
-        serve(6)
-        gather_a(g - 1)
-        data_rows(g, 4, 2)
-        serve(7)
-        b_exchange(g)
-        gather_core(g - 1)
-        data_rows(g, 6, 2)
-        return 0
-
-    lax.fori_loop(1, NF + 1, phase, 0)
-    x_exchange(NF)
-    finish(NF)
-    write_out(NF - 1)
-    gather_b(NF)
-    gather_a(NF)
-    gather_core(NF)
-    write_out(NF)
+
+    def prepare():
+        ld_cout.wait()
+        turn_rows()
+        ld_inp.start()
+        clear_x()
+
+    def load_done():
+        ld_inp.wait()
+        for cp in ld_cw:
+            cp.wait()
+
+    stages = (
+        core_send, core_sum, a_exchange, b_exchange, x_exchange, finish, gather_b, gather_a, gather_core, write_out
+    )
+    plan = {}
+
+    def at(tick, action, *args):
+        plan.setdefault(tick, []).append((action, args))
+
+    at(0, part_chunk, 1, 0)
+    at(1, prepare)
+    at(2, proj_block, 0)
+    at(2, proj_block, 1)
+    at(3, proj_block, 2)
+    at(4, part_chunk, 2, 0)
+    at(5, load_done)
+    for i in range(NB):
+        at((5, 5, 6, 6, 6, 7, 7, 7)[i], gelu, i)
+    for f in range(NF):
+        base = NB * (f + 1)
+        at(base, weight_tap, f, 1, mid)
+        at(base + 1, weight_tap, f, tap_q, mid_q)
+        at(base + X_TICK if f < NF - 1 else base + 3, x_tap, f)
+    for g in range(NF + 1):
+        for n, tick in enumerate(TICKS[g]):
+            at(tick, stages[n], g)
+    for f in range(NF):
+        for i in range(4):
+            at((NB * (f + 1) + X_TICK if f < NF - 1 else 27) + i, data_rows, f, 2 * i, 2)
+    for tick in range(max(NT + LAG - 1, max(plan)) + 1):
+        if tick < NT:
+            service(tick)
+        if LAG <= tick < NT + LAG:
+            forward_x(tick - LAG)
+        for action, args in plan.get(tick, ()):
+            action(*args)
 
     wait_for(part, e_send)
     wait_for(mid, q_send)
@@ -513,7 +485,7 @@
             rows_bf, rows_bf, pltpu.VMEM((CH, ROWS), BF), pltpu.VMEM((ROWS, CH), F32),
             pltpu.VMEM((FULL, CH), BF), pltpu.VMEM((NF, 3, CH, FW), BF),
             chunks, chunks, chunks, chunks, pltpu.VMEM((ROWS, CH), F32),
-            pltpu.VMEM((2, 2, SLAB, 128), F32), pltpu.VMEM((ZP, 128), F32),
+            pltpu.VMEM((2, SLAB, 128), F32), pltpu.VMEM((slabs, ZH, 128), F32), pltpu.VMEM((slabs, ZP, 128), F32),
             pltpu.VMEM((slabs, SLAB, 128), BF), pltpu.VMEM((slabs, SLAB, 128), BF),
             pltpu.VMEM((slabs, ZH, 128), BF), pltpu.VMEM((slabs, ZH, 128), BF),
             pltpu.VMEM((slabs, ZP, 128), BF), pltpu.VMEM((slabs, ZP, 128), BF),

time: 192 us -> 165 us (0.86)
  Pallas kernels: 184 us -> 156 us
    pallas_call x1, Pallas kernels: 184 us -> 156 us  [shards(): pl.pallas_call(kernel, out_shape=(jax.ShapeDtypeStruct((ROWS, CH), BF), j...]
where the time goes in v3:
time: 165 us; the launch traced here: 164 us
  Pallas kernels  156 us (95%)
  local copies, waits for them, and re-layouts  7.02 us (4%)
    pallas_call x1, Pallas kernels, shards(): pl.pallas_call(kernel, out_shape=(jax.ShapeDtypeStruct((ROWS, CH), BF), j...  156 us
    unnamed x7, local copies, waits for them, and re-layouts  7.02 us

profile of v3, /device:TPU:1, one launch (start us, length us, event | category | flops | bytes accessed | tf_op | source)
XLA Modules:
  0.0 164.1 jit_solution(7796969314949910374)
XLA Ops:
  0.6 156.5 %shard_map.76 = (bf16[2048,768]{1,0:T(8,128)(2,1)}, bf16[32,72,768]{2,1,0:T(8,128)(2,1)}, bf16[32,24,768]{2,1,0:T(8,128)(2,1)}) custom-call(bf16[2048,768]{1,0:T(8,128)(2,1)} %bitcast.7, bf16[2048,768]{1,0:T(8,128)(2,1)} %bitcast.8, bf16[2048,768]{1,0:T(8,128)(2,1)} %bitcast.9, bf16[3,768,768]{2,1,0:T(8,128)(2,1)} %cw_h.1, bf16[768,768]{1,0:T(8,128)(2,1)} %pw_h.1), custom_call_target="tpu_custom_call" | custom-call | tf_op jit(solution)/shard_map/pallas_call | solution.py:475
  157.1 0.0 copy-start
  157.1 3.9 %copy.11 = bf16[2,1024,768]{2,1,0:T(8,128)(2,1)} copy(bf16[2,1024,768]{2,1,0:T(8,128)(2,1)} %bitcast.10) | data formatting | bytes 6291456
  161.0 0.0 copy-done
  161.0 0.0 copy-start.1
  161.0 1.8 %copy.12 = bf16[3,768,768]{2,1,0:T(8,128)(2,1)} copy(bf16[3,768,768]{2,1,0:T(8,128)(2,1)S(1)} %bitcast.6) | data formatting | bytes 7077888
  162.8 0.3 copy-done.1
  163.1 1.0 copy.13
Async XLA Ops:
  157.1 3.9 %copy-start = (bf16[32,72,768]{2,1,0:T(8,128)(2,1)S(1)}, bf16[32,72,768]{2,1,0:T(8,128)(2,1)}, u32[]{:S(2)}) copy-start(bf16[32,72,768]{2,1,0:T(8,128)(2,1)} %get-tuple-element.7) | copy-start | bytes 10616836
  161.0 2.1 %copy-start.1 = (bf16[32,24,768]{2,1,0:T(8,128)(2,1)S(1)}, bf16[32,24,768]{2,1,0:T(8,128)(2,1)}, u32[]{:S(2)}) copy-start(bf16[32,24,768]{2,1,0:T(8,128)(2,1)} %get-tuple-element.8) | copy-start | bytes 3538948

commit v4 on v3

--- a/solution.py
+++ b/solution.py
@@ -21,9 +21,9 @@
 LAG = 2
 X_TICK = 5
 TICKS = (
-    (3, 5, 22, 24, 25, 26, 27, 28, 29, 30),
-    (13, 15, 22, 24, 25, 26, 27, 28, 29, 30),
-    (21, 23, 24, 25, 26, 27, 28, 29, 30, 31),
+    (3, 5, 28, 29, 30, 31, 32, 33, 34, 35),
+    (13, 15, 28, 29, 30, 31, 32, 33, 34, 35),
+    (21, 23, 26, 28, 29, 30, 31, 32, 33, 34),
     (27, 28, 28, 29, 30, 31, 32, 33, 34, 35),
 )
 AXES = (0, 1, 0, 1)
@@ -431,12 +431,12 @@
         at(base, weight_tap, f, 1, mid)
         at(base + 1, weight_tap, f, tap_q, mid_q)
         at(base + X_TICK if f < NF - 1 else base + 3, x_tap, f)
-    for g in range(NF + 1):
+    for g in (3, 0, 1, 2):
         for n, tick in enumerate(TICKS[g]):
             at(tick, stages[n], g)
     for f in range(NF):
         for i in range(4):
-            at((NB * (f + 1) + X_TICK if f < NF - 1 else 27) + i, data_rows, f, 2 * i, 2)
+            at((NB * (f + 1) + X_TICK if f < NF - 1 else 28) + i, data_rows, f, 2 * i, 2)
     for tick in range(max(NT + LAG - 1, max(plan)) + 1):
         if tick < NT:
             service(tick)

time: 165 us -> 142 us (0.86)
  Pallas kernels: 156 us -> 134 us
    pallas_call x1, Pallas kernels: 156 us -> 134 us  [shards(): pl.pallas_call(kernel, out_shape=(jax.ShapeDtypeStruct((ROWS, CH), BF), j...]
where the time goes in v4:
time: 142 us; the launch traced here: 141 us
  Pallas kernels  134 us (94%)
  local copies, waits for them, and re-layouts  7.02 us (5%)
    pallas_call x1, Pallas kernels, shards(): pl.pallas_call(kernel, out_shape=(jax.ShapeDtypeStruct((ROWS, CH), BF), j...  134 us
    unnamed x7, local copies, waits for them, and re-layouts  7.02 us

profile of v4, /device:TPU:1, one launch (start us, length us, event | category | flops | bytes accessed | tf_op | source)
XLA Modules:
  0.0 141.5 jit_solution(16408274869264682850)
XLA Ops:
  0.6 133.8 %shard_map.76 = (bf16[2048,768]{1,0:T(8,128)(2,1)}, bf16[32,72,768]{2,1,0:T(8,128)(2,1)}, bf16[32,24,768]{2,1,0:T(8,128)(2,1)}) custom-call(bf16[2048,768]{1,0:T(8,128)(2,1)} %bitcast.7, bf16[2048,768]{1,0:T(8,128)(2,1)} %bitcast.8, bf16[2048,768]{1,0:T(8,128)(2,1)} %bitcast.9, bf16[3,768,768]{2,1,0:T(8,128)(2,1)} %cw_h.1, bf16[768,768]{1,0:T(8,128)(2,1)} %pw_h.1), custom_call_target="tpu_custom_call" | custom-call | tf_op jit(solution)/shard_map/pallas_call | solution.py:475
  134.4 0.0 copy-start
  134.4 3.9 %copy.11 = bf16[2,1024,768]{2,1,0:T(8,128)(2,1)} copy(bf16[2,1024,768]{2,1,0:T(8,128)(2,1)} %bitcast.10) | data formatting | bytes 6291456
  138.3 0.0 copy-done
  138.4 0.0 copy-start.1
  138.4 1.8 %copy.12 = bf16[3,768,768]{2,1,0:T(8,128)(2,1)} copy(bf16[3,768,768]{2,1,0:T(8,128)(2,1)S(1)} %bitcast.6) | data formatting | bytes 7077888
  140.1 0.3 copy-done.1
  140.5 1.0 copy.13
Async XLA Ops:
  134.4 3.9 %copy-start = (bf16[32,72,768]{2,1,0:T(8,128)(2,1)S(1)}, bf16[32,72,768]{2,1,0:T(8,128)(2,1)}, u32[]{:S(2)}) copy-start(bf16[32,72,768]{2,1,0:T(8,128)(2,1)} %get-tuple-element.7) | copy-start | bytes 10616836
  138.4 2.1 %copy-start.1 = (bf16[32,24,768]{2,1,0:T(8,128)(2,1)S(1)}, bf16[32,24,768]{2,1,0:T(8,128)(2,1)}, u32[]{:S(2)}) copy-start(bf16[32,24,768]{2,1,0:T(8,128)(2,1)} %get-tuple-element.8) | copy-start | bytes 3538948
